TPU v7x, 256 devices: a whole 4x4x8 slice. The times are simulated.
256 devices in a mesh: tm: 32 (over y, z), space: 8 (over x, core).
Axes of the slice: x: 4, y: 4, z: 8, core: 2. Of those that a mesh axis runs over, the one named last changes fastest.
Arguments:
- inverse_factor: bfloat16 [2, 32, 4096, 4096], P(None, 'tm', 'space'), may hold values from -1.5 to 1.5, as said below
- tile_mask: int32 [32, 32], replicated, may hold values 0 or 1
- carry_rate: float32 [32, 4096, 2], P('tm', 'space'), may hold values from 0 to 1
- right_side: float32 [32, 4096, 2, 128], P('tm', 'space'), may hold values from -1.5 to 1.5
- arrow_rows: bfloat16 [32, 4096, 2, 512], P('tm', 'space'), may hold values from -0.0625 to 0.0625
- fixed_rhs: float32 [2, 512, 128], P(None, ('tm', 'space')), may hold values from -6 to 6
- tip_factor: bfloat16 [2, 512, 512], replicated, may hold values from -1 to 1, as said below
Outputs:
- solution: float32 [32, 4096, 2, 128], P('tm', 'space')
- fixed_solution: float32 [2, 512, 128], P(None, ('tm', 'space'))
Inputs may be any that keep to these rules, and one draw needn't show every extreme that they name: `tile_mask`: 1 marks a tile that may be nonzero. `inverse_factor`: only entries on or below the diagonal are read. `tip_factor`: only entries on or below the diagonal are read.
All inputs are finite; a program needn't handle non-finite values.
Results may differ from a plain program's by a relative error of at most 0.022.
Values may be sent and summed in bfloat16 or wider, within the bound.
No kernel may reach another device: no remote copies, remote signals or barrier semaphores. Data moves between devices by JAX's collectives and lax.ppermute only.
A program may use at most 320 MiB of HBM per device.

v0:
```python
import jax
import jax.numpy as jnp
from jax import lax
from jax.sharding import PartitionSpec as P

TILE = 128


def carried_in(shard, axis, join, neutral, backward):
    count = lax.axis_size(axis)
    place = lax.axis_index(axis)
    ahead = count - 1 - place if backward else place
    gathered = jax.tree.map(
        lambda a, kind: lax.all_gather(a.astype(kind), axis), shard, (jnp.bfloat16, jnp.bfloat16)
    )
    state = jax.tree.map(lambda a, e: jnp.zeros_like(a) + jnp.asarray(e, a.dtype), shard, neutral)

    def one(turn, state):
        source = count - 1 - turn if backward else turn
        return join(
            state,
            jax.tree.map(
                lambda a, own: lax.dynamic_index_in_dim(a, source, 0, False).astype(own.dtype),
                gathered,
                shard,
            ),
        )

    return lax.fori_loop(0, ahead, one, state)


def combine(earlier, latter):
    rate_new = latter[0] * earlier[0]
    rest = tuple(
        (value_l + latter[0] * value_e for value_l, value_e in zip(latter[1:], earlier[1:]))
    )
    return (rate_new,) + rest


def tile_keep(tile_table, row_start, row_total, col_total):
    tile_count = tile_table.shape[0]
    tile_ids = jnp.arange(tile_count, dtype=jnp.int32)
    row_index = row_start + jnp.arange(row_total, dtype=jnp.int32)
    col_index = jnp.arange(col_total, dtype=jnp.int32)
    row_onehot = (row_index[:, None] // TILE == tile_ids[None, :]).astype(jnp.float32)
    col_onehot = (col_index[:, None] // TILE == tile_ids[None, :]).astype(jnp.float32)
    marked = jnp.dot(jnp.dot(row_onehot, tile_table.astype(jnp.float32)), col_onehot.T)
    return (marked > 0.5) & (row_index[:, None] >= col_index[None, :])


def on_device(inverse_factor, tile_mask, carry_rate, right_side, arrow_rows, fixed_rhs, tip_factor):
    row_count = right_side.shape[1]
    node_total = inverse_factor.shape[3]
    row_start = lax.axis_index("space") * row_count
    tile_table = jnp.maximum(tile_mask, jnp.eye(tile_mask.shape[0], dtype=jnp.int32))
    weights = inverse_factor[:, 0]
    bf_zero = jnp.zeros((), jnp.bfloat16)
    rate_col = carry_rate[0][:, :, None]
    source = right_side[0]
    unit_rate = jnp.ones_like(rate_col)
    earlier_sum = carried_in(
        (rate_col, source), "tm", combine, (unit_rate, jnp.zeros_like(source)), False
    )
    forward = source + rate_col * earlier_sum[1]
    forward_b = forward.astype(jnp.bfloat16)
    row_keep = tile_keep(tile_table, row_start, row_count, node_total)
    masked_rows = jnp.where(row_keep[None], weights, bf_zero)
    block = masked_rows
    inner_rows = jnp.einsum(
        "hrn,nhk->rhk",
        block,
        lax.all_gather(forward_b, "space", axis=0, tiled=True),
        preferred_element_type=jnp.float32,
    ).astype(jnp.bfloat16)
    block = masked_rows
    scaled = lax.psum_scatter(
        jnp.einsum("hrn,rhk->nhk", block, inner_rows, preferred_element_type=jnp.float32).astype(
            jnp.bfloat16
        ),
        "space",
        scatter_dimension=0,
        tiled=True,
    ).astype(jnp.float32)
    arrow_part = arrow_rows[0]
    coupling = jnp.einsum("rhf,rhk->hfk", arrow_part, forward_b, preferred_element_type=jnp.float32)
    share_rows = fixed_rhs.shape[1]
    share_start = lax.axis_index(("tm", "space")) * share_rows
    contrib = -coupling
    own_part = lax.dynamic_slice_in_dim(contrib, share_start, share_rows, 1) + fixed_rhs
    contrib = lax.dynamic_update_slice_in_dim(contrib, own_part, share_start, 1)
    fixed_forward = lax.psum(contrib, ("tm", "space")).astype(jnp.bfloat16)
    fixed_total = tip_factor.shape[1]
    fixed_index = jnp.arange(fixed_total, dtype=jnp.int32)
    lower_tri = fixed_index[:, None] >= fixed_index[None, :]
    tip_lower = jnp.where(lower_tri[None], tip_factor, bf_zero)
    tip_inner = jnp.einsum(
        "hij,hjk->hik", tip_lower, fixed_forward, preferred_element_type=jnp.float32
    ).astype(jnp.bfloat16)
    fixed_solution = jnp.einsum(
        "hij,hik->hjk", tip_lower, tip_inner, preferred_element_type=jnp.float32
    )
    fixed_own = lax.dynamic_slice_in_dim(fixed_solution, share_start, share_rows, 1)
    fixed_b = fixed_solution.astype(jnp.bfloat16)
    carried = scaled - jnp.einsum(
        "rhf,hfk->rhk", arrow_part, fixed_b, preferred_element_type=jnp.float32
    )
    following = carried_in(
        (rate_col, rate_col * carried), "tm", combine, (unit_rate, jnp.zeros_like(carried)), True
    )
    solution = carried + following[1]
    return (solution[None], fixed_own)


def solution(mesh):
    placed = (
        P(None, "tm", "space", None),
        P(),
        P("tm", "space", None),
        P("tm", "space", None, None),
        P("tm", "space", None, None),
        P(None, ("tm", "space"), None),
        P(),
    )
    return jax.shard_map(
        on_device,
        mesh=mesh,
        in_specs=placed,
        out_specs=(P("tm", "space", None, None), P(None, ("tm", "space"), None)),
        check_vma=False,
    )
```

profile of v0, /device:TPU:2, one launch (start us, length us, event | category | flops | bytes accessed | tf_op | source)
XLA Modules:
  0.0 596.0 jit_solution(12626880782622736189)
XLA Ops:
  7.2 1.9 copy.62
  9.2 1.2 copy.34
  11.1 52.1 %all-gather = bf16[32,512,2]{1,2,0:T(2,128)(2,1)S(1)} all-gather(bf16[1,512,2]{1,2,0:T(2,128)(2,1)S(1)} %convert_element_type.103), channel_id=2, replica_groups=mesh['tm'=32,'space'=8] {'tm'}, dimensions={0}, use_global_device_ids=true | all-gather | bytes 67584 | tf_op jit(solution)/shard_map/all_gather | solution.py:14
  63.2 3.3 copy.37
  66.6 46.1 %all-gather.6.cloned.1.call-done = bf16[32,512,2,128]{3,1,2,0:T(8,128)(2,1)} async-done(((bf16[1,512,2,128]{3,1,2,0:T(8,128)(2,1)}), bf16[32,512,2,128]{3,1,2,0:T(8,128)(2,1)}) %all-gather.6.cloned.1.call-update) | async-done | bytes 8388624 | tf_op jit(solution)/shard_map/all_gather | solution.py:14
  114.4 4.2 fusion
  118.6 154.2 %all-gather.8.cloned.1.call-done = bf16[4096,2,128]{0,2,1:T(8,128)(2,1)} async-done(((bf16[512,2,128]{0,2,1:T(8,128)(2,1)}), bf16[4096,2,128]{0,2,1:T(8,128)(2,1)}) %all-gather.8.cloned.1.call-update) | async-done | bytes 2097168 | tf_op jit(solution)/shard_map/all_gather | solution.py:72
  272.7 13.2 %fusion.4 = bf16[4096,2,128]{0,2,1:T(8,128)(2,1)} fusion(bf16[2,1,512,4096]{3,2,1,0:T(8,128)(2,1)} %param.11, pred[512,4096]{1,0:T(8,128)(4,1)} %fusion, bf16[4096,2,128]{0,2,1:T(8,128)(2,1)} %all-gather.8.cloned.1.call-done), kind=kOutput, calls=%fused_computation.12 | convolution fusion | flops 2157051904 | bytes 14680064 | tf_op jit(solution)/shard_map/hrn,rhk->nhk/dot_general | solution.py:77
  286.7 1.1 dynamic_update_slice.3
  287.8 78.9 %all-reduce.1 = bf16[2,512,128]{1,2,0:T(8,128)(2,1)S(1)} all-reduce(f32[2,512,128]{1,2,0:T(8,128)S(1)} %dynamic_update_slice.3), channel_id=1, replica_groups=mesh['tm'=32,'space'=8] {'tm','space'}, use_global_device_ids=true, to_apply=%region_3.4 | all-reduce | flops 131072 | bytes 786432 | tf_op jit(solution)/shard_map/psum | solution.py:91
  366.7 2.3 fusion.9
  369.0 2.1 multiply_convert_fusion
  371.8 102.9 %all-gather.10.cloned.1.call-done = bf16[16384,2,128]{0,2,1:T(8,128)(2,1)} async-done(((bf16[512,2,128]{0,2,1:T(8,128)(2,1)}), bf16[16384,2,128]{0,2,1:T(8,128)(2,1)}) %all-gather.10.cloned.1.call-update) | async-done | bytes 8388624 | tf_op jit(solution)/shard_map/all_gather | solution.py:14
  474.7 21.1 %copy.52 = bf16[16384,2,128]{2,1,0:T(2,128)(2,1)} copy(bf16[16384,2,128]{0,2,1:T(8,128)(2,1)} %all-gather.10.cloned.1.call-done) | data formatting | bytes 16777216 | tf_op jit(solution)/shard_map/while | solution.py:29
  495.9 92.2 %while.27 = (s32[]{:T(128)}, f32[512,2,128]{2,1,0:T(2,128)S(1)}, s32[]{:T(128)}, bf16[32,512,2,128]{3,2,1,0:T(2,128)(2,1)}, bf16[32,512,2,1]{2,1,3,0:T(8,128)(2,...) while((s32[]{:T(128)}, f32[512,2,128]{2,1,0:T(2,128)S(1)}, s32[]{:T(128)}, ...), condition=%wide.region_5.6_spmd, body=%wide.region_4.5_spmd.sunk | while | flops 394246 | bytes 1321107 | solution.py:29
  495.9 0.9 bitcast_convert_fusion.5
  496.9 2.0 convert_add_fusion.5
  499.8 2.0 convert_add_fusion.5
  502.8 2.0 convert_add_fusion.5
  505.8 2.0 convert_add_fusion.5
  508.8 2.0 convert_add_fusion.5
  511.7 2.0 convert_add_fusion.5
  514.7 2.0 convert_add_fusion.5
  517.7 2.0 convert_add_fusion.5
  520.7 2.0 convert_add_fusion.5
  523.6 2.0 convert_add_fusion.5
  526.6 2.0 convert_add_fusion.5
  529.6 2.0 convert_add_fusion.5
  532.6 2.0 convert_add_fusion.5
  535.5 2.0 convert_add_fusion.5
  538.5 2.0 convert_add_fusion.5
  541.5 2.0 convert_add_fusion.5
  544.5 2.0 convert_add_fusion.5
  547.4 2.0 convert_add_fusion.5
  550.4 2.0 convert_add_fusion.5
  553.4 2.0 convert_add_fusion.5
  556.3 2.0 convert_add_fusion.5
  559.3 2.0 convert_add_fusion.5
  562.3 2.0 convert_add_fusion.5
  565.3 2.0 convert_add_fusion.5
  568.2 2.0 convert_add_fusion.5
  571.2 2.0 convert_add_fusion.5
  574.2 2.0 convert_add_fusion.5
  577.2 2.0 convert_add_fusion.5
  580.1 2.0 convert_add_fusion.5
  583.1 2.0 convert_add_fusion.5
  586.1 2.0 convert_add_fusion.5
  588.4 1.0 copy.48
  (64 shorter events, 32.1 us)
Async XLA Ops:
  7.2 279.1 %copy-start = (bf16[1,512,2,512]{3,2,1,0:T(2,128)(2,1)S(1)}, bf16[1,512,2,512]{3,2,1,0:T(2,128)(2,1)}, u32[]{:S(2)}) copy-start(bf16[1,512,2,512]{3,2,1,0:T(2,128)(2,1)} %param.15) | copy-start | bytes 3145732
  7.2 105.5 %all-gather.6.cloned.1.call-start = ((), (), s32[]{:S(2)}) async-start(), calls=%async_computation.1 | async-start | bytes 8650752 | tf_op jit(solution)/shard_map/all_gather | solution.py:14
  9.1 263.6 %all-gather.8.cloned.1.call-start = ((), (), s32[]{:S(2)}) async-start(), calls=%async_computation.2 | async-start | bytes 2359296 | tf_op jit(solution)/shard_map/all_gather | solution.py:72
  112.8 0.7 copy-start.2
  112.8 1.6 copy-start.4
  114.3 254.7 %reduce-scatter.2.cloned.1.call-start = ((), (), s32[]{:S(2)}) async-start(), calls=%async_computation.3 | async-start | bytes 2359296 | tf_op jit(solution)/shard_map/reduce_scatter | solution.py:76
  118.6 167.5 %copy-start.3 = (f32[2,2,128]{2,1,0:T(2,128)S(1)}, f32[2,2,128]{2,1,0:T(2,128)}, u32[]{:S(2)}) copy-start(f32[2,2,128]{2,1,0:T(2,128)} %param.16) | copy-start | bytes 6148
  118.6 167.7 %copy-start.1 = (bf16[512,2,128]{0,2,1:T(8,128)(2,1)S(1)}, bf16[512,2,128]{0,2,1:T(8,128)(2,1)}, u32[]{:S(2)}) copy-start(bf16[512,2,128]{0,2,1:T(8,128)(2,1)} %fusion.19) | copy-start | bytes 786436
  286.0 188.7 %all-gather.10.cloned.1.call-start = ((), (), s32[]{:S(2)}) async-start(), calls=%async_computation.4 | async-start | bytes 8650752 | tf_op jit(solution)/shard_map/all_gather | solution.py:14
Sparse Core Ops, SparseCore 0:
  11.2 101.4 all-gather.5
  115.0 157.6 all-gather.7
  286.1 34.6 reduce-scatter.1
  371.3 103.2 all-gather.9
where the time goes:
time: 598 us; the launch traced here: 596 us
  waiting for transfers between devices  303 us (51%)
  blocking collectives  131 us (22%)
  other arithmetic  92.9 us (16%)
  local copies, waits for them, and re-layouts  31.4 us (5%)
  matrix products  22.2 us (4%)
  between operations  14 us (2%)
    all_gather x1, waiting for transfers between devices, on_device(): lax.all_gather(forward_b, 'space', axis=0, tiled=True)  154 us
    all_gather x2, waiting for transfers between devices, carried_in(): lax.all_gather(a.astype(kind), axis)  149 us
    psum x1, blocking collectives, on_device(): fixed_forward = lax.psum(contrib, ('tm', 'space')).astype(jnp.bfloat16)  78.9 us
    add x31, other arithmetic, combine(): value_l + latter[0] * value_e  62.3 us
    all_gather x1, blocking collectives, carried_in(): lax.all_gather(a.astype(kind), axis)  52.1 us
    convert_element_type x31, other arithmetic, one(): lax.dynamic_index_in_dim(a, source, 0, False).astype(own.dtype)  28.8 us
    while x4, local copies, waits for them, and re-layouts, carried_in(): return lax.fori_loop(0, ahead, one, state)  24.8 us
    dot_general x1, matrix products, on_device(): jnp.einsum('hrn,rhk->nhk', block, inner_rows, preferred_element_type=jnp....  13.2 us
  transfers between devices with their start and end apart: 4, of which 3 were waited for; matrix products, arithmetic and copies ran while one was open for 2% of the time, Pallas kernels for 0%

commit v1 on v0

--- a/solution.py
+++ b/solution.py
@@ -4,6 +4,22 @@
 from jax.sharding import PartitionSpec as P
 
 TILE = 128
+
+
+def ring_product(x, axis, dim, term):
+    size, position, width = (lax.axis_size(axis), lax.axis_index(axis), x.shape[dim])
+    right = [(i, (i + 1) % size) for i in range(size)]
+    left = [(i, (i - 1) % size) for i in range(size)]
+    middle = size // 2
+    from_left = from_right = x
+    total = term(x, position * width)
+    for step in range(1, middle + 1):
+        from_left = lax.ppermute(from_left, axis, right)
+        if step < size - middle:
+            from_right = lax.ppermute(from_right, axis, left)
+            total = total + term(from_right, (position + step) % size * width)
+        total = total + term(from_left, (position - step) % size * width)
+    return total
 
 
 def carried_in(shard, axis, join, neutral, backward):
@@ -66,11 +82,16 @@
     row_keep = tile_keep(tile_table, row_start, row_count, node_total)
     masked_rows = jnp.where(row_keep[None], weights, bf_zero)
     block = masked_rows
-    inner_rows = jnp.einsum(
-        "hrn,nhk->rhk",
-        block,
-        lax.all_gather(forward_b, "space", axis=0, tiled=True),
-        preferred_element_type=jnp.float32,
+    inner_rows = ring_product(
+        forward_b,
+        "space",
+        0,
+        lambda part, at: jnp.einsum(
+            "hrn,nhk->rhk",
+            lax.dynamic_slice_in_dim(block, at, part.shape[0], axis=2),
+            part,
+            preferred_element_type=jnp.float32,
+        ),
     ).astype(jnp.bfloat16)
     block = masked_rows
     scaled = lax.psum_scatter(

time: 598 us -> 596 us (level)
  waiting for transfers between devices: 303 us -> 147 us
  blocking collectives: 131 us -> 266 us
  other arithmetic: 92.9 us -> 101 us
    all_gather x1 -> x0, waiting for transfers between devices: 154 us -> none  [on_device(): lax.all_gather(forward_b, 'space', axis=0, tiled=True)]
    psum x1, blocking collectives: 78.9 us -> 214 us  [on_device(): fixed_forward = lax.psum(contrib, ('tm', 'space')).astype(jnp.bfloat16)]
    dot_general x0 -> x7, matrix products: none -> 11.9 us  [on_device(): jnp.einsum('hrn,nhk->rhk', lax.dynamic_slice_in_dim(block, at, part.shape...]
    select_n x0 -> x1, other arithmetic: none -> 8.49 us  [on_device(): masked_rows = jnp.where(row_keep[None], weights, bf_zero)]
    dot_general x1, matrix products: 13.2 us -> 6.71 us  [on_device(): jnp.einsum('hrn,rhk->nhk', block, inner_rows, preferred_element_type=jnp....]
  transfers between devices with their start and end apart: 4 -> 10, of which waited for: 3 -> 5; matrix products, arithmetic and copies ran while one was open for 2% -> 6% of each run, Pallas kernels for 0% -> 0%
where the time goes in v1:
time: 596 us; the launch traced here: 593 us
  blocking collectives  266 us (45%)
  waiting for transfers between devices  147 us (25%)
  other arithmetic  101 us (17%)
  local copies, waits for them, and re-layouts  31 us (5%)
  matrix products  28 us (5%)
  between operations  14 us (2%)
    psum x1, blocking collectives, on_device(): fixed_forward = lax.psum(contrib, ('tm', 'space')).astype(jnp.bfloat16)  214 us
    all_gather x2, waiting for transfers between devices, carried_in(): lax.all_gather(a.astype(kind), axis)  143 us
    add x31, other arithmetic, combine(): value_l + latter[0] * value_e  62.3 us
    all_gather x1, blocking collectives, carried_in(): lax.all_gather(a.astype(kind), axis)  52.1 us
    convert_element_type x31, other arithmetic, one(): lax.dynamic_index_in_dim(a, source, 0, False).astype(own.dtype)  28.7 us
    while x4, local copies, waits for them, and re-layouts, carried_in(): return lax.fori_loop(0, ahead, one, state)  24.8 us
  transfers between devices with their start and end apart: 10, of which 5 were waited for; matrix products, arithmetic and copies ran while one was open for 6% of the time, Pallas kernels for 0%

profile of v1, /device:TPU:2, one launch (start us, length us, event | category | flops | bytes accessed | tf_op | source)
XLA Modules:
  0.0 593.4 jit_solution(5634916871451262593)
XLA Ops:
  7.2 1.9 copy.62
  11.1 52.1 %all-gather = bf16[32,512,2]{1,2,0:T(2,128)(2,1)S(1)} all-gather(bf16[1,512,2]{1,2,0:T(2,128)(2,1)S(1)} %convert_element_type.100), channel_id=2, replica_groups=mesh['tm'=32,'space'=8] {'tm'}, dimensions={0}, use_global_device_ids=true | all-gather | bytes 67584 | tf_op jit(solution)/shard_map/all_gather | solution.py:30
  63.2 3.3 copy.37
  66.6 4.6 fusion
  71.2 41.4 %all-gather.5.cloned.1.call-done = bf16[32,512,2,128]{3,1,2,0:T(8,128)(2,1)} async-done(((bf16[1,512,2,128]{3,1,2,0:T(8,128)(2,1)}), bf16[32,512,2,128]{3,1,2,0:T(8,128)(2,1)}) %all-gather.5.cloned.1.call-update) | async-done | bytes 8388624 | tf_op jit(solution)/shard_map/all_gather | solution.py:30
  113.2 1.7 collective-permute-start
  114.9 8.5 %bitcast_select_fusion = bf16[2,512,4096]{2,1,0:T(8,128)(2,1)} fusion(bf16[2,1,512,4096]{3,2,1,0:T(8,128)(2,1)} %param.11, pred[512,4096]{1,0:T(8,128)(4,1)} %fusion), kind=kLoop, calls=%fused_computation.6 | loop fusion | flops 4194304 | bytes 18874368 | tf_op jit(solution)/shard_map/jit(_where)/select_n | solution.py:83
  125.1 1.7 collective-permute-start.2
  130.9 2.0 collective-permute-start.4
  140.1 2.4 collective-permute-done.6
  142.5 6.7 %fusion.1 = bf16[4096,2,128]{0,2,1:T(8,128)(2,1)} fusion(bf16[2,512,4096]{2,1,0:T(8,128)(2,1)} %bitcast_select_fusion, f32[2,128,512]{2,1,0:T(8,128)S(1)} %fusion.3, bf16[512,2,128]{0,2,1:T(8,128)(2,1)S(1)} %collective-permute-done.6, s32[]{:T(128)S(6)} %select_n.122), kind=kOutput, calls=%fused_computation.10 | convolution fusion | flops 1209270272 | bytes 12320772 | tf_op jit(solution)/shard_map/hrn,rhk->nhk/dot_general | solution.py:98
  151.0 214.3 %all-reduce.1 = bf16[2,512,128]{1,2,0:T(8,128)(2,1)S(1)} all-reduce(f32[2,512,128]{1,2,0:T(8,128)S(1)} %dynamic_update_slice.3), channel_id=1, replica_groups=mesh['tm'=32,'space'=8] {'tm','space'}, use_global_device_ids=true, to_apply=%region_3.4 | all-reduce | flops 131072 | bytes 786432 | tf_op jit(solution)/shard_map/psum | solution.py:112
  365.3 2.3 fusion.6
  367.7 2.1 multiply_convert_fusion
  370.4 101.9 %all-gather.7.cloned.1.call-done = bf16[16384,2,128]{0,2,1:T(8,128)(2,1)} async-done(((bf16[512,2,128]{0,2,1:T(8,128)(2,1)}), bf16[16384,2,128]{0,2,1:T(8,128)(2,1)}) %all-gather.7.cloned.1.call-update) | async-done | bytes 8388624 | tf_op jit(solution)/shard_map/all_gather | solution.py:30
  472.3 21.1 %copy.52 = bf16[16384,2,128]{2,1,0:T(2,128)(2,1)} copy(bf16[16384,2,128]{0,2,1:T(8,128)(2,1)} %all-gather.7.cloned.1.call-done) | data formatting | bytes 16777216 | tf_op jit(solution)/shard_map/while | solution.py:45
  493.5 92.0 %while.27 = (s32[]{:T(128)}, f32[512,2,128]{2,1,0:T(2,128)S(1)}, s32[]{:T(128)}, bf16[32,512,2,128]{3,2,1,0:T(2,128)(2,1)}, bf16[32,512,2,1]{2,1,3,0:T(8,128)(2,...) while((s32[]{:T(128)}, f32[512,2,128]{2,1,0:T(2,128)S(1)}, s32[]{:T(128)}, ...), condition=%wide.region_5.6_spmd, body=%wide.region_4.5_spmd.sunk | while | flops 394246 | bytes 1321115 | solution.py:45
  494.5 2.0 convert_add_fusion.5
  497.4 2.0 convert_add_fusion.5
  500.4 2.0 convert_add_fusion.5
  503.4 2.0 convert_add_fusion.5
  506.4 2.0 convert_add_fusion.5
  509.3 2.0 convert_add_fusion.5
  512.3 2.0 convert_add_fusion.5
  515.3 2.0 convert_add_fusion.5
  518.2 2.0 convert_add_fusion.5
  521.2 2.0 convert_add_fusion.5
  524.2 2.0 convert_add_fusion.5
  527.1 2.0 convert_add_fusion.5
  530.1 2.0 convert_add_fusion.5
  533.1 2.0 convert_add_fusion.5
  536.0 2.0 convert_add_fusion.5
  539.0 2.0 convert_add_fusion.5
  542.0 2.0 convert_add_fusion.5
  544.9 2.0 convert_add_fusion.5
  547.9 2.0 convert_add_fusion.5
  550.9 2.0 convert_add_fusion.5
  553.9 2.0 convert_add_fusion.5
  556.8 2.0 convert_add_fusion.5
  559.8 2.0 convert_add_fusion.5
  562.8 2.0 convert_add_fusion.5
  565.7 2.0 convert_add_fusion.5
  568.7 2.0 convert_add_fusion.5
  571.7 2.0 convert_add_fusion.5
  574.6 2.0 convert_add_fusion.5
  577.6 2.0 convert_add_fusion.5
  580.6 2.0 convert_add_fusion.5
  583.5 2.0 convert_add_fusion.5
  (79 shorter events, 48.0 us)
Async XLA Ops:
  7.2 142.4 %copy-start = (bf16[1,512,2,512]{3,2,1,0:T(2,128)(2,1)S(1)}, bf16[1,512,2,512]{3,2,1,0:T(2,128)(2,1)}, u32[]{:S(2)}) copy-start(bf16[1,512,2,512]{3,2,1,0:T(2,128)(2,1)} %param.15) | copy-start | bytes 3145732
  7.2 105.5 %all-gather.5.cloned.1.call-start = ((), (), s32[]{:S(2)}) async-start(), calls=%async_computation.1 | async-start | bytes 8650752 | tf_op jit(solution)/shard_map/all_gather | solution.py:30
  9.1 358.5 %reduce-scatter.2.cloned.1.call-start = ((), (), s32[]{:S(2)}) async-start(), calls=%async_computation.2 | async-start | bytes 2359296 | tf_op jit(solution)/shard_map/reduce_scatter | solution.py:97
  71.2 41.8 %copy-start.1 = (f32[1,512,2]{1,2,0:T(2,128)S(1)}, f32[1,512,2]{1,2,0:T(2,128)}, u32[]{:S(2)}) copy-start(f32[1,512,2]{1,2,0:T(2,128)} %param.13) | copy-start | bytes 12292
  113.1 11.9 %collective-permute-start.1 = (bf16[512,2,128]{0,2,1:T(8,128)(2,1)S(1)}, bf16[512,2,128]{0,2,1:T(8,128)(2,1)S(1)}, u32[]{:S(2)}, u32[]{:S(2)}) collective-permute-start(bf16[512,2,128]{0,2,1:T(8,128)(2,1)S(1)} %fusion.28), channel_id=1, source_target_pairs={{0,1},{1,2},{2,3},{3,4},{4,5},{5,6},{6,7},{7,0},{8,9},{9,10},{10,1... | collective-permute-start | bytes 786440 | tf_op jit(solution)/shard_map/ppermute | solution.py:17
  113.2 12.0 %collective-permute-start = (bf16[512,2,128]{0,2,1:T(8,128)(2,1)S(1)}, bf16[512,2,128]{0,2,1:T(8,128)(2,1)S(1)}, u32[]{:S(2)}, u32[]{:S(2)}) collective-permute-start(bf16[512,2,128]{0,2,1:T(8,128)(2,1)S(1)} %fusion.28), channel_id=1, source_target_pairs={{0,7},{1,0},{2,1},{3,2},{4,3},{5,4},{6,5},{7,6},{8,15},{9,8},{10,9... | collective-permute-start | bytes 786440 | tf_op jit(solution)/shard_map/ppermute | solution.py:19
  125.1 5.8 collective-permute-start.3
  125.1 5.8 collective-permute-start.2
  130.9 5.8 collective-permute-start.5
  130.9 7.5 %collective-permute-start.4 = (bf16[512,2,128]{0,2,1:T(8,128)(2,1)S(1)}, bf16[512,2,128]{0,2,1:T(8,128)(2,1)S(1)}, u32[]{:S(2)}, u32[]{:S(2)}) collective-permute-start(bf16[512,2,128]{0,2,1:T(8,128)(2,1)S(1)} %collective-permute-done.2), channel_id=1, source_target_pairs={{0,7},{1,0},{2,1},{3,2},{4,3},{5,4},{6,5},{7,6},{8,15},{9,8},{10,9... | collective-permute-start | bytes 786440 | tf_op jit(solution)/shard_map/ppermute | solution.py:19
  136.7 5.8 collective-permute-start.6
  138.4 10.9 %copy-start.2 = (f32[2,2,128]{2,1,0:T(2,128)S(1)}, f32[2,2,128]{2,1,0:T(2,128)}, u32[]{:S(2)}) copy-start(f32[2,2,128]{2,1,0:T(2,128)} %param.16) | copy-start | bytes 6148
  149.2 323.1 %all-gather.7.cloned.1.call-start = ((), (), s32[]{:S(2)}) async-start(), calls=%async_computation.3 | async-start | bytes 8650752 | tf_op jit(solution)/shard_map/all_gather | solution.py:30
Sparse Core Ops, SparseCore 0:
  11.2 101.4 all-gather.4
  149.4 167.5 reduce-scatter.1
  370.0 102.2 all-gather.6
